TPU v7x, 32 devices: a whole 2x2x4 slice. The times are simulated.
32 devices in a mesh: rows: 8 (over y, x, core), cols: 4 (over z).
Axes of the slice: x: 2, y: 2, z: 4, core: 2. Of those that a mesh axis runs over, the one named last changes fastest.
Arguments:
- coords: int32 [8, 16384], P(None, ('rows', 'cols')), may hold values from 0 to 4095
- probes: float32 [64, 16384], P(None, ('rows', 'cols')), may hold values from -6 to 6
- lengthscales: float32 [8], replicated, may hold values from 0.15 to 0.25
- amplitude: float32 [1], replicated, may hold values from 0.1 to 0.3
- landmarks: float32 [14, 8, 128], replicated, may hold values from 0 to 1
- coupling: float32 [128, 128], replicated, may hold values from -0.5 to 0.5
Outputs:
- products: float32 [2, 64, 16384], P(None, None, ('rows', 'cols'))
All inputs are finite; a program needn't handle non-finite values.
Results may differ from a plain program's by a relative error of at most 0.0025.
Values may be sent and summed in bfloat16 or wider, within the bound.
A program may use at most 64 MiB of HBM per device.

v0:
```python
import jax
import jax.numpy as jnp
from jax import lax
from jax.sharding import PartitionSpec as P


def swapped(array, axis, apart):
    return lax.ppermute(array, axis, [(i, i ^ 1 << apart) for i in range(lax.axis_size(axis))])


def pair_squares(left_points, right_points):
    squared = jnp.zeros((left_points.shape[1], right_points.shape[1]), jnp.float32)
    for component in range(left_points.shape[0]):
        offset = left_points[component][:, None] - right_points[component][None, :]
        squared = squared + offset * offset
    return squared


def on_device(coords, probes, lengthscales, amplitude, landmarks, coupling):
    highest = lax.Precision.HIGHEST
    inverse_scale = 1.0 / lengthscales
    scaled = coords.astype(jnp.float32) * (1.0 / 4096.0) * inverse_scale[:, None]
    strength = amplitude[0]
    signs_half = probes.astype(jnp.bfloat16)
    width = coords.shape[1]
    groups = lax.axis_size("cols")
    rows_index = lax.axis_index("rows")
    levels = lax.axis_size("rows").bit_length() - 1
    leaf_points = lax.all_gather(scaled, "cols", axis=1, tiled=True)
    leaf_signs = lax.all_gather(signs_half, "cols", axis=1, tiled=True)
    accumulated = jnp.zeros((2, probes.shape[0], width), jnp.float32)
    for row_block in range(groups):
        block_points = leaf_points[:, row_block * width : (row_block + 1) * width]
        block_signs = leaf_signs[:, row_block * width : (row_block + 1) * width]
        squared = pair_squares(block_points, scaled)
        kernel = strength * jnp.exp(-0.5 * squared)
        kernel_half = kernel.astype(jnp.bfloat16)
        slope_half = (kernel * squared).astype(jnp.bfloat16)
        accumulated = accumulated + jnp.stack(
            [
                jnp.dot(block_signs, kernel_half, preferred_element_type=jnp.float32),
                jnp.dot(block_signs, slope_half, preferred_element_type=jnp.float32),
            ]
        )
    result = accumulated
    factor_list = []
    dfactor_list = []
    for level in range(levels):
        depth = levels - level
        node = jnp.right_shift(rows_index, level)
        chosen = lax.dynamic_index_in_dim(landmarks, 2**depth - 2 + node, 0, keepdims=False)
        squared = pair_squares(scaled, chosen * inverse_scale[:, None])
        factor = strength * jnp.exp(-0.5 * squared)
        factor_list.append(factor)
        dfactor_list.append(factor * squared)
    factor_stack = jnp.stack(factor_list)
    dfactor_stack = jnp.stack(dfactor_list)
    own_project = jnp.einsum("pn,lnr->lpr", probes, factor_stack, precision=highest)
    own_dproject = jnp.einsum("pn,lnr->lpr", probes, dfactor_stack, precision=highest)
    projections = lax.psum(jnp.stack([own_project, own_dproject], axis=1), "cols")
    siblings = []
    pending = projections
    for level in range(levels):
        partner = swapped(pending[level:], "rows", level)
        siblings.append(partner[0])
        pending = pending.at[level + 1 :].add(partner[1:])
    for level in range(levels):
        sibling_sums = siblings[level]
        is_left = jnp.right_shift(rows_index, level) & 1 == 0
        core = jnp.where(is_left, coupling.T, coupling)
        first = jnp.dot(sibling_sums[0], core, precision=highest)
        second = jnp.dot(sibling_sums[1], core, precision=highest)
        value = jnp.dot(first, factor_stack[level].T, precision=highest)
        slope = jnp.dot(first, dfactor_stack[level].T, precision=highest) + jnp.dot(
            second, factor_stack[level].T, precision=highest
        )
        result = result + jnp.stack([value, slope])
    return result


def solution(mesh):
    in_specs = (P(None, ("rows", "cols")), P(None, ("rows", "cols")), P(), P(), P(), P())
    out_specs = P(None, None, ("rows", "cols"))
    return jax.shard_map(
        on_device, mesh=mesh, in_specs=in_specs, out_specs=out_specs, check_vma=False
    )
```

profile of v0, /device:TPU:0, one launch (start us, length us, event | category | flops | bytes accessed | tf_op | source)
XLA Modules:
  0.0 75.2 jit_solution(17061877505005976449)
XLA Ops:
  6.5 0.0 copy-start.3
  6.5 0.0 all-reduce.2.cloned.1.call-start
  6.5 0.0 copy-start.4
  6.5 0.7 copy-done.4
  7.2 0.0 copy-done.3
  7.3 0.1 convert_multiply_fusion
  8.0 0.8 %bitcast_multiply_fusion.2 = (f32[8,128]{1,0:T(8,128)S(1)}, f32[8,128]{1,0:T(8,128)S(1)}, f32[8,128]{1,0:T(8,128)S(1)}) fusion(f32[14,8,128]{2,1,0:T(8,128)} %param.14, s32[]{:T(128)S(6)} %select_n.30, f32[8]{0:T(128)S(1)} %get-tuple-element.30, s32[]{:T(128)S(6)} %select_n.32, s32[]{:T(128)S(6)} %select_n.31), kind=kLoop, calls=%fused_computation.137 | loop fusion | flops 3072 | bytes 24620 | tf_op jit(solution)/shard_map/mul | solution.py:52
  8.8 0.6 exponential_multiply_fusion.17
  9.4 0.6 exponential_multiply_fusion.16
  10.1 0.0 copy-start.1
  10.1 0.6 exponential_multiply_fusion.18
  10.7 0.3 copy-done.1
  11.0 0.6 convolution_bitcast_fusion.12
  11.6 0.6 convolution_bitcast_fusion.11
  12.1 0.7 pad_maximum_fusion
  12.8 0.0 all-reduce.2.cloned.1.call-update
  12.9 15.0 %all_gather.6 = f32[8,2048]{1,0:T(8,128)S(1)} all-gather(f32[8,512]{1,0:T(8,128)S(1)} %convert_multiply_fusion), channel_id=1, replica_groups=mesh['rows'=8,'cols'=4] {'cols'}, dimensions={1}, use_global_device_ids=true | all-gather | bytes 81920 | tf_op jit(solution)/shard_map/all_gather | solution.py:29
  27.9 0.0 copy-start
  28.0 0.8 %copy-done = f32[128,128]{1,0:T(8,128)S(1)} copy-done((f32[128,128]{1,0:T(8,128)S(1)}, f32[128,128]{1,0:T(8,128)}, u32[]{:S(2)}) %copy-start) | copy-done | bytes 65560
  28.8 0.1 copy.7
  28.9 14.7 %all_gather.7 = bf16[64,2048]{1,0:T(8,128)(2,1)S(1)} all-gather(bf16[64,512]{1,0:T(8,128)(2,1)S(1)} %convert_element_type.32), channel_id=1, replica_groups=mesh['rows'=8,'cols'=4] {'cols'}, dimensions={1}, use_global_device_ids=true | all-gather | bytes 327680 | tf_op jit(solution)/shard_map/all_gather | solution.py:30
  43.5 1.1 %convolution_bitcast_fusion.1 = f32[1,64,512]{2,1,0:T(8,128)S(1)} fusion(f32[]{:T(128)} %bitcast.196, f32[512]{0:T(512)S(1)} %bitcast.393, f32[512]{0:T(512)S(1)} %bitcast.395, f32[512]{0:T(512)S(1)} %bitcast.397, f32[512]{0:T(512)S(1)} %bitcast.399, f32[512]{0:T(512)S(1)} %bitcast.401, f32[512]{0:T(512)S(1)} %bitcast.403, f32[512]{0:T(512)S(1)} %bitcast.405, ...), kind=kOutput, calls=%fused_computation.1 | convolution fusion | flops 40370176 | bytes 229380 | tf_op jit(solution)/shard_map/dot_general | solution.py:41
  44.7 1.2 %convolution_bitcast_fusion = f32[1,64,512]{2,1,0:T(8,128)S(1)} fusion(f32[]{:T(128)} %bitcast.195, f32[512]{0:T(512)S(1)} %bitcast.394, f32[512]{0:T(512)S(1)} %bitcast.396, f32[512]{0:T(512)S(1)} %bitcast.398, f32[512]{0:T(512)S(1)} %bitcast.400, f32[512]{0:T(512)S(1)} %bitcast.402, f32[512]{0:T(512)S(1)} %bitcast.404, f32[512]{0:T(512)S(1)} %bitcast.406, ...), kind=kOutput, calls=%fused_computation | convolution fusion | flops 40632320 | bytes 229380 | tf_op jit(solution)/shard_map/dot_general | solution.py:42
  45.9 1.1 %convolution_bitcast_fusion.3 = f32[1,64,512]{2,1,0:T(8,128)S(1)} fusion(f32[]{:T(128)} %bitcast.197, f32[512]{0:T(512)S(1)} %bitcast.375, f32[512]{0:T(512)S(1)} %bitcast.377, f32[512]{0:T(512)S(1)} %bitcast.379, f32[512]{0:T(512)S(1)} %bitcast.381, f32[512]{0:T(512)S(1)} %bitcast.383, f32[512]{0:T(512)S(1)} %bitcast.385, f32[512]{0:T(512)S(1)} %bitcast.387, ...), kind=kOutput, calls=%fused_computation.3 | convolution fusion | flops 40370176 | bytes 229380 | tf_op jit(solution)/shard_map/dot_general | solution.py:41
  47.1 1.2 %convolution_bitcast_fusion.2 = f32[1,64,512]{2,1,0:T(8,128)S(1)} fusion(f32[]{:T(128)} %bitcast.194, f32[512]{0:T(512)S(1)} %bitcast.376, f32[512]{0:T(512)S(1)} %bitcast.378, f32[512]{0:T(512)S(1)} %bitcast.380, f32[512]{0:T(512)S(1)} %bitcast.382, f32[512]{0:T(512)S(1)} %bitcast.384, f32[512]{0:T(512)S(1)} %bitcast.386, f32[512]{0:T(512)S(1)} %bitcast.388, ...), kind=kOutput, calls=%fused_computation.2 | convolution fusion | flops 40632320 | bytes 229380 | tf_op jit(solution)/shard_map/dot_general | solution.py:42
  48.3 1.1 %convolution_bitcast_fusion.5 = f32[1,64,512]{2,1,0:T(8,128)S(1)} fusion(f32[]{:T(128)} %bitcast.198, f32[512]{0:T(512)S(1)} %bitcast.369, f32[512]{0:T(512)S(1)} %bitcast.371, f32[512]{0:T(512)S(1)} %bitcast.373, f32[512]{0:T(512)S(1)} %bitcast.425, f32[512]{0:T(512)S(1)} %bitcast.427, f32[512]{0:T(512)S(1)} %bitcast.429, f32[512]{0:T(512)S(1)} %bitcast.431, ...), kind=kOutput, calls=%fused_computation.5 | convolution fusion | flops 40370176 | bytes 229380 | tf_op jit(solution)/shard_map/dot_general | solution.py:41
  49.4 1.2 %convolution_bitcast_fusion.4 = f32[1,64,512]{2,1,0:T(8,128)S(1)} fusion(f32[]{:T(128)} %bitcast.193, f32[512]{0:T(512)S(1)} %bitcast.370, f32[512]{0:T(512)S(1)} %bitcast.372, f32[512]{0:T(512)S(1)} %bitcast.374, f32[512]{0:T(512)S(1)} %bitcast.426, f32[512]{0:T(512)S(1)} %bitcast.428, f32[512]{0:T(512)S(1)} %bitcast.430, f32[512]{0:T(512)S(1)} %bitcast.432, ...), kind=kOutput, calls=%fused_computation.4 | convolution fusion | flops 40632320 | bytes 229380 | tf_op jit(solution)/shard_map/dot_general | solution.py:42
  50.6 1.1 %convolution_bitcast_fusion.7 = f32[1,64,512]{2,1,0:T(8,128)S(1)} fusion(f32[]{:T(128)} %bitcast.189, f32[512]{0:T(512)S(1)} %bitcast.238, f32[512]{0:T(512)S(1)} %bitcast.407, f32[512]{0:T(512)S(1)} %bitcast.258, f32[512]{0:T(512)S(1)} %bitcast.409, f32[512]{0:T(512)S(1)} %bitcast.278, f32[512]{0:T(512)S(1)} %bitcast.411, f32[512]{0:T(512)S(1)} %bitcast.298, ...), kind=kOutput, calls=%fused_computation.7 | convolution fusion | flops 40370176 | bytes 229380 | tf_op jit(solution)/shard_map/dot_general | solution.py:41
  51.8 0.0 all-reduce.2.cloned.1.call-done
  51.8 0.1 collective-permute-start
  51.9 0.0 copy-start.2
  51.9 1.2 %convolution_bitcast_fusion.6 = f32[1,64,512]{2,1,0:T(8,128)S(1)} fusion(f32[]{:T(128)} %bitcast.192, f32[512]{0:T(512)S(1)} %bitcast.239, f32[512]{0:T(512)S(1)} %bitcast.408, f32[512]{0:T(512)S(1)} %bitcast.259, f32[512]{0:T(512)S(1)} %bitcast.410, f32[512]{0:T(512)S(1)} %bitcast.279, f32[512]{0:T(512)S(1)} %bitcast.412, f32[512]{0:T(512)S(1)} %bitcast.299, ...), kind=kOutput, calls=%fused_computation.6 | convolution fusion | flops 40632320 | bytes 229380 | tf_op jit(solution)/shard_map/dot_general | solution.py:42
  53.1 0.4 collective-permute-done
  53.5 0.0 copy-done.2
  53.6 1.3 %collective-permute-start.1 = (f32[2,2,64,128]{3,2,0,1:T(8,128)S(1)}, f32[2,2,64,128]{3,2,0,1:T(8,128)S(1)}, u32[]{:S(2)}, u32[]{:S(2)}) collective-permute-start(f32[2,2,64,128]{3,2,0,1:T(8,128)S(1)} %slice_add_fusion), channel_id=1, source_target_pairs={{0,8},{4,12},{8,0},{12,4},{16,24},{20,28},{24,16},{28,20},{1,9},{5... | collective-permute-start | bytes 393224 | tf_op jit(solution)/shard_map/ppermute | solution.py:8
  54.9 0.2 fusion.84
  55.1 1.0 %fusion.46 = f32[64,512]{1,0:T(8,128)S(1)} fusion(f32[64,128]{1,0:T(8,128)S(1)} %fusion.84, f32[]{:T(128)} %bitcast.199, f32[128]{0:T(128)S(1)} %get-tuple-element.81, f32[512]{0:T(512)S(1)} %bitcast.240, f32[128]{0:T(128)S(1)} %get-tuple-element.82, f32[512]{0:T(512)S(1)} %bitcast.260, f32[128]{0:T(128)S(1)} %get-tuple-element.83, f32[512]{0:T(512)S(1)} %bitcast.280, ...), kind=kOutput, calls=%fused_computation.75 | convolution fusion | flops 52035584 | bytes 184324 | tf_op jit(solution)/shard_map/dot_general | solution.py:74
  56.1 0.2 fusion.83
  56.3 1.0 %fusion.2 = f32[1,64,512]{2,1,0:T(8,128)S(1)} fusion(f32[64,512]{1,0:T(8,128)S(1)} %fusion.46, f32[64,128]{1,0:T(8,128)S(1)} %fusion.83, f32[]{:T(128)} %bitcast.200, f32[128]{0:T(128)S(1)} %get-tuple-element.81, f32[512]{0:T(512)S(1)} %bitcast.241, f32[128]{0:T(128)S(1)} %get-tuple-element.82, f32[512]{0:T(512)S(1)} %bitcast.261, ...), kind=kOutput, calls=%fused_computation.16 | convolution fusion | flops 52002816 | bytes 315396 | tf_op jit(solution)/shard_map/dot_general | solution.py:74
  57.3 1.0 %convolution_bitcast_fusion.10 = f32[1,64,512]{2,1,0:T(8,128)S(1)} fusion(f32[64,128]{1,0:T(8,128)S(1)} %fusion.84, f32[]{:T(128)} %bitcast.191, f32[128]{0:T(128)S(1)} %get-tuple-element.81, f32[512]{0:T(512)S(1)} %bitcast.242, f32[128]{0:T(128)S(1)} %get-tuple-element.82, f32[512]{0:T(512)S(1)} %bitcast.262, f32[128]{0:T(128)S(1)} %get-tuple-element.83, ...), kind=kOutput, calls=%fused_computation.10 | convolution fusion | flops 51970048 | bytes 184324 | tf_op jit(solution)/shard_map/dot_general | solution.py:73
  58.2 0.9 %collective-permute-done.1 = f32[2,2,64,128]{3,2,0,1:T(8,128)S(1)} collective-permute-done((f32[2,2,64,128]{3,2,0,1:T(8,128)S(1)}, f32[2,2,64,128]{3,2,0,1:T(8,128)S(1)}, u32[]{:S(2)}, u32[]{:S(2)}) %collective-permute-start.1) | collective-permute-done | bytes 131104 | tf_op jit(solution)/shard_map/ppermute | solution.py:8
  59.2 1.4 %collective-permute-start.2 = (f32[1,2,64,128]{3,2,0,1:T(8,128)S(1)}, f32[1,2,64,128]{3,2,0,1:T(8,128)S(1)}, u32[]{:S(2)}, u32[]{:S(2)}) collective-permute-start(f32[1,2,64,128]{3,2,0,1:T(8,128)S(1)} %slice_add_fusion.1), channel_id=1, source_target_pairs={{0,16},{4,20},{8,24},{12,28},{16,0},{20,4},{24,8},{28,12},{1,17},{... | collective-permute-start | bytes 196616 | tf_op jit(solution)/shard_map/ppermute | solution.py:8
  60.6 0.2 fusion.82
  60.7 1.2 %fusion.44 = f32[64,512]{1,0:T(8,128)S(1)} fusion(f32[64,128]{1,0:T(8,128)S(1)} %fusion.82, f32[]{:T(128)} %bitcast.201, f32[128]{0:T(128)S(1)} %get-tuple-element.110, f32[128]{0:T(128)S(1)} %get-tuple-element.109, f32[128]{0:T(128)S(1)} %get-tuple-element.108, f32[128]{0:T(128)S(1)} %get-tuple-element.107, f32[128]{0:T(128)S(1)} %get-tuple-element.106, ...), kind=kOutput, calls=%fused_computation.71 | convolution fusion | flops 52035584 | bytes 184324 | tf_op jit(solution)/shard_map/dot_general | solution.py:74
  62.0 0.2 fusion.81
  62.1 1.0 %fusion.1 = f32[1,64,512]{2,1,0:T(8,128)S(1)} fusion(f32[64,512]{1,0:T(8,128)S(1)} %fusion.44, f32[64,128]{1,0:T(8,128)S(1)} %fusion.81, f32[]{:T(128)} %bitcast.202, f32[128]{0:T(128)S(1)} %get-tuple-element.110, f32[128]{0:T(128)S(1)} %get-tuple-element.109, f32[128]{0:T(128)S(1)} %get-tuple-element.108, f32[128]{0:T(128)S(1)} %get-tuple-element.107, ...), kind=kOutput, calls=%fused_computation.14 | convolution fusion | flops 52002816 | bytes 315396 | tf_op jit(solution)/shard_map/dot_general | solution.py:74
  63.1 1.0 %convolution_bitcast_fusion.9 = f32[1,64,512]{2,1,0:T(8,128)S(1)} fusion(f32[64,128]{1,0:T(8,128)S(1)} %fusion.82, f32[]{:T(128)} %bitcast.206, f32[128]{0:T(128)S(1)} %get-tuple-element.110, f32[128]{0:T(128)S(1)} %get-tuple-element.109, f32[128]{0:T(128)S(1)} %get-tuple-element.108, f32[128]{0:T(128)S(1)} %get-tuple-element.107, ...), kind=kOutput, calls=%fused_computation.9 | convolution fusion | flops 51970048 | bytes 184324 | tf_op jit(solution)/shard_map/dot_general | solution.py:73
  64.1 0.0 collective-permute-done.2
  64.1 0.2 fusion.80
  64.3 1.0 %convolution_bitcast_fusion.8 = f32[1,64,512]{2,1,0:T(8,128)S(1)} fusion(f32[64,128]{1,0:T(8,128)S(1)} %fusion.80, f32[]{:T(128)} %bitcast.205, f32[128]{0:T(128)S(1)} %get-tuple-element.97, f32[128]{0:T(128)S(1)} %get-tuple-element.98, f32[128]{0:T(128)S(1)} %get-tuple-element.99, f32[128]{0:T(128)S(1)} %get-tuple-element.100, ...), kind=kOutput, calls=%fused_computation.8 | convolution fusion | flops 51970048 | bytes 184324 | tf_op jit(solution)/shard_map/dot_general | solution.py:73
  65.3 1.0 %fusion.42 = f32[64,512]{1,0:T(8,128)S(1)} fusion(f32[64,128]{1,0:T(8,128)S(1)} %fusion.80, f32[]{:T(128)} %bitcast.203, f32[128]{0:T(128)S(1)} %get-tuple-element.97, f32[128]{0:T(128)S(1)} %get-tuple-element.98, f32[128]{0:T(128)S(1)} %get-tuple-element.99, f32[128]{0:T(128)S(1)} %get-tuple-element.100, f32[128]{0:T(128)S(1)} %get-tuple-element.101, ...), kind=kOutput, calls=%fused_computation.67 | convolution fusion | flops 52035584 | bytes 184324 | tf_op jit(solution)/shard_map/dot_general | solution.py:74
  66.3 0.2 fusion.79
  66.5 1.0 %fusion = f32[1,64,512]{2,1,0:T(8,128)S(1)} fusion(f32[64,512]{1,0:T(8,128)S(1)} %fusion.42, f32[64,128]{1,0:T(8,128)S(1)} %fusion.79, f32[]{:T(128)} %bitcast.204, f32[128]{0:T(128)S(1)} %get-tuple-element.97, f32[128]{0:T(128)S(1)} %get-tuple-element.98, f32[128]{0:T(128)S(1)} %get-tuple-element.99, f32[128]{0:T(128)S(1)} %get-tuple-element.100, ...), kind=kOutput, calls=%fused_computation.12 | convolution fusion | flops 52002816 | bytes 315396 | tf_op jit(solution)/shard_map/dot_general | solution.py:74
  67.5 0.9 %fusion.41 = f32[2,64,512]{2,1,0:T(8,128)} fusion(f32[1,64,512]{2,1,0:T(8,128)S(1)} %convolution_bitcast_fusion.6, f32[1,64,512]{2,1,0:T(8,128)S(1)} %convolution_bitcast_fusion.7, f32[1,64,512]{2,1,0:T(8,128)S(1)} %convolution_bitcast_fusion.4, f32[1,64,512]{2,1,0:T(8,128)S(1)} %convolution_bitcast_fusion.5, ...), kind=kLoop, calls=%fused_computation.66 | loop fusion | flops 851968 | bytes 2097152 | tf_op jit(solution)/shard_map/add | solution.py:77
  (9 shorter events, 0.1 us)
Async XLA Ops:
  6.5 0.7 copy-start.3
  6.5 45.3 %all-reduce.2.cloned.1.call-start = ((), (), s32[]{:S(2)}) async-start(), calls=%async_computation | async-start | bytes 393216 | tf_op jit(solution)/shard_map/psum | solution.py:60
  6.5 0.7 copy-start.4
  10.1 0.9 %copy-start.1 = (f32[64,512]{1,0:T(8,128)S(1)}, f32[64,512]{1,0:T(8,128)}, u32[]{:S(2)}) copy-start(f32[64,512]{1,0:T(8,128)} %param.11) | copy-start | bytes 393220
  27.9 0.8 %copy-start = (f32[128,128]{1,0:T(8,128)S(1)}, f32[128,128]{1,0:T(8,128)}, u32[]{:S(2)}) copy-start(f32[128,128]{1,0:T(8,128)} %param.15) | copy-start | bytes 196612
  51.8 1.7 %collective-permute-start = (f32[3,2,64,128]{3,2,0,1:T(8,128)}, f32[3,2,64,128]{3,2,0,1:T(8,128)S(1)}, u32[]{:S(2)}, u32[]{:S(2)}) collective-permute-start(f32[3,2,64,128]{3,2,0,1:T(8,128)} %all-reduce.2.cloned.1.call-done), channel_id=1, source_target_pairs={{0,4},{4,0},{8,12},{12,8},{16,20},{20,16},{24,28},{28,24},{1,5},{5... | collective-permute-start | bytes 589832 | tf_op jit(solution)/shard_map/ppermute | solution.py:8
  51.9 1.6 %copy-start.2 = (f32[3,2,64,128]{3,2,0,1:T(8,128)S(1)}, f32[3,2,64,128]{3,2,0,1:T(8,128)}, u32[]{:S(2)}) copy-start(f32[3,2,64,128]{3,2,0,1:T(8,128)} %all-reduce.2.cloned.1.call-done) | copy-start | bytes 589828
  53.6 5.6 %collective-permute-start.1 = (f32[2,2,64,128]{3,2,0,1:T(8,128)S(1)}, f32[2,2,64,128]{3,2,0,1:T(8,128)S(1)}, u32[]{:S(2)}, u32[]{:S(2)}) collective-permute-start(f32[2,2,64,128]{3,2,0,1:T(8,128)S(1)} %slice_add_fusion), channel_id=1, source_target_pairs={{0,8},{4,12},{8,0},{12,4},{16,24},{20,28},{24,16},{28,20},{1,9},{5... | collective-permute-start | bytes 393224 | tf_op jit(solution)/shard_map/ppermute | solution.py:8
  59.2 4.9 %collective-permute-start.2 = (f32[1,2,64,128]{3,2,0,1:T(8,128)S(1)}, f32[1,2,64,128]{3,2,0,1:T(8,128)S(1)}, u32[]{:S(2)}, u32[]{:S(2)}) collective-permute-start(f32[1,2,64,128]{3,2,0,1:T(8,128)S(1)} %slice_add_fusion.1), channel_id=1, source_target_pairs={{0,16},{4,20},{8,24},{12,28},{16,0},{20,4},{24,8},{28,12},{1,17},{... | collective-permute-start | bytes 196616 | tf_op jit(solution)/shard_map/ppermute | solution.py:8
Sparse Core Ops, SparseCore 0:
  13.0 38.0 all-reduce.1
where the time goes:
time: 75.5 us; the launch traced here: 75.2 us
  blocking collectives  29.7 us (39%)
  matrix products  20.8 us (28%)
  between operations  14.3 us (19%)
  other arithmetic  4.35 us (6%)
  starting transfers between devices  2.77 us (4%)
  local copies, waits for them, and re-layouts  1.91 us (3%)
  waiting for transfers between devices  1.38 us (2%)
    all_gather x1, blocking collectives, on_device(): leaf_points = lax.all_gather(scaled, 'cols', axis=1, tiled=True)  15 us
    all_gather x1, blocking collectives, on_device(): leaf_signs = lax.all_gather(signs_half, 'cols', axis=1, tiled=True)  14.7 us
    dot_general x4, matrix products, on_device(): jnp.dot(block_signs, slope_half, preferred_element_type=jnp.float32)  4.86 us
    dot_general x4, matrix products, on_device(): jnp.dot(block_signs, kernel_half, preferred_element_type=jnp.float32)  4.57 us
    dot_general x3, matrix products, on_device(): jnp.dot(first, dfactor_stack[level].T, precision=highest)  3.17 us
    dot_general x3, matrix products, on_device(): jnp.dot(second, factor_stack[level].T, precision=highest)  2.95 us
    dot_general x3, matrix products, on_device(): value = jnp.dot(first, factor_stack[level].T, precision=highest)  2.95 us
    ppermute x3, starting transfers between devices, swapped(): lax.ppermute(array, axis, [(i, i ^ 1 << apart) for i in range(lax.axis_si...  2.77 us
  transfers between devices with their start and end apart: 4, of which 2 were waited for; matrix products, arithmetic and copies ran while one was open for 22% of the time, Pallas kernels for 0%

commit v1 on v0

v1 whole, which is shorter than its diff:
```python
import functools
import math

import jax
import jax.numpy as jnp
from jax import lax
from jax.experimental import pallas as pl
from jax.experimental.pallas import tpu as pltpu
from jax.sharding import PartitionSpec as P

F32 = jnp.float32
BF16 = jnp.bfloat16
HALF_LOG2E = 0.5 / math.log(2.0)
UNIT = HALF_LOG2E / 4096.0**2
MESH = pl.DeviceIdType.MESH
LANES = 128


def toggled(index, mask):
    bit = 1
    while bit <= mask:
        if mask & bit:
            index = index + bit - 2 * bit * ((index // bit) % 2)
        bit *= 2
    return index


def halves(x):
    high = x.astype(BF16)
    return high, (x - high.astype(F32)).astype(BF16)


def thirds(x):
    first = x.astype(BF16).astype(F32)
    rest = x - first
    second = rest.astype(BF16).astype(F32)
    return first, second, rest - second


def rows_of(pieces, shape):
    at = lax.broadcasted_iota(jnp.int32, shape, 0)
    out = jnp.zeros(shape, F32)
    for i, piece in enumerate(pieces):
        out = jnp.where(at == i, piece, out)
    return out


def padded(groups):
    n = groups[0].shape[1]
    rest = LANES - sum(g.shape[0] for g in groups)
    return jnp.concatenate(groups + [jnp.zeros((rest, n), F32)], axis=0)


def dot(a, b):
    return jnp.dot(a, b, preferred_element_type=F32)


def dot_t(a, b):
    return lax.dot_general(a, b, (((1,), (1,)), ((), ())), preferred_element_type=F32)


def kernel(
    groups, levels,
    scale_ref, amp_ref, coords_ref, probes_ref, land_ref, coup_ref, out_ref,
    half, cbuf, pbuf, lhs, fac, grown, proj, send_a, recv_a, send_b, recv_b,
    gs_sem, gr_sem, as_sem, ar_sem, bs_sem, br_sem,
):
    row, col = lax.axis_index("rows"), lax.axis_index("cols")
    width = coords_ref.shape[1]
    probes = probes_ref.shape[0]
    rank = coup_ref.shape[0]

    targets = []
    for level in range(1, levels):
        for m in range(2 ** (level - 1)):
            targets.append((level, (1 << level) ^ (2 * m)))
    peers = [(row, toggled(col, k)) for k in range(1, groups)]
    peers.append((toggled(row, 1), col))
    peers += [(toggled(row, mask), col) for _, mask in targets]

    barrier = pltpu.get_barrier_semaphore()
    for peer in peers:
        pl.semaphore_signal(barrier, inc=1, device_id=peer, device_id_type=MESH)
    half[...] = probes_ref[...].astype(BF16)
    pl.semaphore_wait(barrier, len(peers))

    gathers = []
    for k in range(1, groups):
        peer = (row, toggled(col, k))
        pair = [
            pltpu.make_async_remote_copy(
                src_ref=src, dst_ref=dst.at[k - 1], send_sem=gs_sem.at[k - 1, i], recv_sem=gr_sem.at[k - 1, i],
                device_id=peer, device_id_type=MESH,
            )
            for i, (src, dst) in enumerate(((coords_ref, cbuf), (half, pbuf)))
        ]
        for copy in pair:
            copy.start()
        gathers.append(pair)

    at = lax.broadcasted_iota(jnp.int32, (8, LANES), 0)
    scales = jnp.ones((8, LANES), F32)
    for d in range(8):
        scales = jnp.where(at == d, scale_ref[d], scales)
    weight = (1.0 / (scales * scales))[:, :1] * UNIT
    log_amp = jnp.log(jnp.full((1, LANES), amp_ref[0], F32)) * (1.0 / math.log(2.0))
    log_amp = log_amp[:, :1]
    offset = log_amp * (1.0 / HALF_LOG2E)
    slant = 1.0 / HALF_LOG2E

    def centred(coords):
        return (coords - 2048).astype(F32)

    own = centred(coords_ref[...])
    anchors = []
    for level in range(levels):
        depth = levels - level
        chosen = land_ref[2**depth - 2 + row // (1 << level)]
        anchors.append((chosen - 0.5) * 4096.0)
    left = jnp.concatenate([own] + anchors, axis=1)
    weighted = weight * left
    y1, y2, y3 = thirds(2.0 * weighted)
    norm = log_amp - jnp.sum(weighted * left, axis=0, keepdims=True)
    ones = jnp.ones_like(norm)
    special = rows_of(list(thirds(norm)) + [ones] * 3, left.shape)
    lhs[...] = jnp.transpose(padded([y1, y1, y2, y2, y3, y3, special])).astype(BF16)

    def features(coords):
        value = centred(coords)
        high = value.astype(BF16).astype(F32)
        low = value - high
        norm = -jnp.sum(weight * value * value, axis=0, keepdims=True)
        ones = jnp.ones_like(norm)
        special = rows_of([ones] * 3 + list(thirds(norm)), value.shape)
        return padded([high, low, high, low, high, low, special]).astype(BF16)

    def pair_of(start, feat):
        power = dot(lhs[start : start + LANES, :], feat)
        kern = jnp.exp2(power)
        return kern, kern * (offset - slant * power)

    def diagonal(feat, signs, first):
        for j in range(0, width, LANES):
            kern, slope = pair_of(j, feat)
            both = jnp.concatenate([kern.astype(BF16), slope.astype(BF16)], axis=0)
            got = dot_t(signs, both)
            for i in range(2):
                part = got[:, i * LANES : (i + 1) * LANES]
                if first:
                    out_ref[i, :, j : j + LANES] = part
                else:
                    out_ref[i, :, j : j + LANES] += part

    def project(feat, signs, first):
        for level in range(levels):
            kern, slope = pair_of(width + level * rank, feat)
            pieces = halves(kern) + halves(slope)
            if first:
                for i in range(4):
                    fac[i, level] = pieces[i]
            got = dot_t(signs, jnp.concatenate(pieces, axis=0))
            for i in range(2):
                part = got[:, 2 * i * rank : (2 * i + 1) * rank] + got[:, (2 * i + 1) * rank : (2 * i + 2) * rank]
                if first:
                    proj[level, i] = part
                else:
                    proj[level, i] += part

    feat = features(coords_ref[...])
    project(feat, half[...], True)
    diagonal(feat, half[...], True)

    coupling = coup_ref[...]
    flipped = jnp.transpose(coupling)
    for level in range(levels):
        side = ((row // (1 << level)) % 2).astype(F32)
        core = jnp.where(jnp.full((rank, rank), side) < 0.5, flipped, coupling)
        high, low = halves(core)
        both = jnp.concatenate([high, low], axis=0)
        for i in range(2):
            got = dot(both, fac[2 * i, level])
            total = got[:rank] + got[rank:] + dot(high, fac[2 * i + 1, level])
            g_high, g_low = halves(total)
            grown[2 * i, level * rank : (level + 1) * rank, :] = g_high
            grown[2 * i + 1, level * rank : (level + 1) * rank, :] = g_low

    for k in range(1, groups):
        for copy in gathers[k - 1]:
            copy.wait_recv()
        feat = features(cbuf[k - 1])
        signs = pbuf[k - 1]
        project(feat, signs, False)
        if k < groups - 1:
            diagonal(feat, signs, False)

    send_a[...] = proj[...].astype(send_a.dtype)
    swap = pltpu.make_async_remote_copy(
        src_ref=send_a, dst_ref=recv_a, send_sem=as_sem, recv_sem=ar_sem,
        device_id=(toggled(row, 1), col), device_id_type=MESH,
    )
    swap.start()
    if groups > 1:
        diagonal(feat, signs, False)
    swap.wait_recv()

    send_b[...] = (proj[1:] + recv_a[1:].astype(F32)).astype(send_b.dtype)
    hops = []
    for i, (level, mask) in enumerate(targets):
        copy = pltpu.make_async_remote_copy(
            src_ref=send_b.at[level - 1], dst_ref=recv_b.at[i], send_sem=bs_sem.at[i], recv_sem=br_sem.at[i],
            device_id=(toggled(row, mask), col), device_id_type=MESH,
        )
        copy.start()
        hops.append(copy)

    def apply(sums, low_row, high_row):
        high, low = halves(sums)
        both = jnp.concatenate([high, low], axis=0)
        g = [grown[i, low_row:high_row, :] for i in range(4)]
        a = dot(both, g[0])
        b = dot(high, g[1])
        c = dot(jnp.concatenate([high[:probes], low[:probes]], axis=0), g[2])
        d = dot(high[:probes], g[3])
        plain = a[: 2 * probes] + a[2 * probes :] + b
        out_ref[0] += plain[:probes]
        out_ref[1] += plain[probes:] + c[:probes] + c[probes:] + d

    apply(jnp.concatenate([recv_a[0, 0], recv_a[0, 1]], axis=0).astype(F32), 0, rank)
    for copy in hops:
        copy.wait_recv()
    sums = []
    for level in range(1, levels):
        total = None
        for i, (at_level, _) in enumerate(targets):
            if at_level == level:
                part = recv_b[i].astype(F32)
                total = part if total is None else total + part
        sums.append(jnp.concatenate([total[0], total[1]], axis=0))
    if sums:
        apply(jnp.concatenate(sums, axis=1), rank, levels * rank)

    for pair in gathers:
        for copy in pair:
            copy.wait_send()
    swap.wait_send()
    for copy in hops:
        copy.wait_send()


def on_device(coords, probes, lengthscales, amplitude, landmarks, coupling):
    groups = lax.axis_size("cols")
    levels = lax.axis_size("rows").bit_length() - 1
    dims, width = coords.shape
    count, rank = probes.shape[0], coupling.shape[0]
    others = max(groups - 1, 1)
    hops = max(2 ** (levels - 1) - 1, 1)
    upper = max(levels - 1, 1)
    vmem = pl.BlockSpec(memory_space=pltpu.VMEM)
    smem = pl.BlockSpec(memory_space=pltpu.SMEM)
    wire = F32
    return pl.pallas_call(
        functools.partial(kernel, groups, levels),
        out_shape=jax.ShapeDtypeStruct((2, count, width), F32),
        in_specs=[smem, smem, vmem, vmem, vmem, vmem],
        out_specs=vmem,
        scratch_shapes=[
            pltpu.VMEM((count, width), BF16),
            pltpu.VMEM((others, dims, width), jnp.int32),
            pltpu.VMEM((others, count, width), BF16),
            pltpu.VMEM((width + levels * rank, LANES), BF16),
            pltpu.VMEM((4, levels, rank, width), BF16),
            pltpu.VMEM((4, levels * rank, width), BF16),
            pltpu.VMEM((levels, 2, count, rank), F32),
            pltpu.VMEM((levels, 2, count, rank), wire),
            pltpu.VMEM((levels, 2, count, rank), wire),
            pltpu.VMEM((upper, 2, count, rank), wire),
            pltpu.VMEM((hops, 2, count, rank), wire),
            pltpu.SemaphoreType.DMA((others, 2)),
            pltpu.SemaphoreType.DMA((others, 2)),
            pltpu.SemaphoreType.DMA,
            pltpu.SemaphoreType.DMA,
            pltpu.SemaphoreType.DMA((hops,)),
            pltpu.SemaphoreType.DMA((hops,)),
        ],
        compiler_params=pltpu.CompilerParams(collective_id=0, has_side_effects=True),
    )(lengthscales, amplitude, coords, probes, landmarks, coupling)


def solution(mesh):
    in_specs = (P(None, ("rows", "cols")), P(None, ("rows", "cols")), P(), P(), P(), P())
    out_specs = P(None, None, ("rows", "cols"))
    return jax.shard_map(
        on_device, mesh=mesh, in_specs=in_specs, out_specs=out_specs, check_vma=False
    )
```

time: 75.5 us -> 27.1 us (0.36)
  blocking collectives: 29.7 us -> 0 us
  Pallas kernels: 0 us -> 24.6 us
  matrix products: 20.8 us -> 0 us
  between operations: 14.3 us -> 0.66 us
  other arithmetic: 4.35 us -> 0 us
  starting transfers between devices: 2.77 us -> 0 us
  waiting for transfers between devices: 1.38 us -> 0 us
    all_gather x2 -> x0, blocking collectives: 29.7 us -> none  [the longest x1 15 us: on_device(): leaf_points = lax.all_gather(scaled, 'cols', axis=1, tiled=True)]
    pallas_call x0 -> x1, Pallas kernels: none -> 24.6 us  [on_device(): pl.pallas_call(functools.partial(kernel, groups, levels), out_shape=jax.S...]
    dot_general x25 -> x0, matrix products: 20.8 us -> none  [the longest x4 4.86 us: on_device(): jnp.dot(block_signs, slope_half, preferred_element_type=jnp.float32)]
    ppermute x3 -> x0, starting transfers between devices: 2.77 us -> none  [swapped(): lax.ppermute(array, axis, [(i, i ^ 1 << apart) for i in range(lax.axis_si...]
    mul x6 -> x0, other arithmetic: 2.74 us -> none  [the longest x3 1.86 us: on_device(): factor = strength * jnp.exp(-0.5 * squared)]
    ppermute x3 -> x0, waiting for transfers between devices: 1.34 us -> none  [swapped(): lax.ppermute(array, axis, [(i, i ^ 1 << apart) for i in range(lax.axis_si...]
    add x3 -> x0, other arithmetic: 0.91 us -> none  [the longest x1 0.89 us: on_device(): result = result + jnp.stack([value, slope])]
    unnamed x11 -> x1, local copies, waits for them, and re-layouts: 1.83 us -> 1.67 us
  transfers between devices with their start and end apart: 4 -> 0, of which waited for: 2 -> 0; matrix products, arithmetic and copies ran while one was open for 22% -> 0% of each run, Pallas kernels for 0% -> 0%
where the time goes in v1:
time: 27.1 us; the launch traced here: 26.9 us
  Pallas kernels  24.6 us (91%)
  local copies, waits for them, and re-layouts  1.67 us (6%)
  between operations  0.66 us (2%)
    pallas_call x1, Pallas kernels, on_device(): pl.pallas_call(functools.partial(kernel, groups, levels), out_shape=jax.S...  24.6 us
    unnamed x1, local copies, waits for them, and re-layouts  1.67 us

profile of v1, /device:TPU:0, one launch (start us, length us, event | category | flops | bytes accessed | tf_op | source)
XLA Modules:
  0.0 26.9 jit_solution(12585390870036377207)
XLA Ops:
  0.7 24.6 %shard_map.64 = f32[2,64,512]{2,1,0:T(8,128)} custom-call(f32[8]{0:T(128)} %scale_ref.1, f32[1]{0:T(128)S(6)} %copy.8.amp_ref, s32[8,512]{1,0:T(8,128)} %coords_ref.1, f32[64,512]{1,0:T(8,128)} %probes_ref.1, f32[14,8,128]{2,1,0:T(8,128)} %land_ref.1, f32[128,128]{1,0:T(8,128)} %coup_ref.1), custom_call_target="tpu_custom_call" | custom-call | tf_op jit(solution)/shard_map/pallas_call | solution.py:261
  25.2 1.7 %copy.9 = f32[2,64,512]{2,1,0:T(8,128)} copy(f32[2,64,512]{2,1,0:T(8,128)} %shard_map.64) | data formatting | bytes 524288

commit v2 on v1

--- a/solution.py
+++ b/solution.py
@@ -62,7 +62,7 @@
 def kernel(
     groups, levels,
     scale_ref, amp_ref, coords_ref, probes_ref, land_ref, coup_ref, out_ref,
-    half, cbuf, pbuf, lhs, fac, grown, proj, send_a, recv_a, send_b, recv_b,
+    half, cbuf, pbuf, lhs, near, fac, grown, proj, send_a, recv_a, send_b, recv_b,
     gs_sem, gr_sem, as_sem, ar_sem, bs_sem, br_sem,
 ):
     row, col = lax.axis_index("rows"), lax.axis_index("cols")
@@ -84,19 +84,15 @@
     half[...] = probes_ref[...].astype(BF16)
     pl.semaphore_wait(barrier, len(peers))
 
-    gathers = []
-    for k in range(1, groups):
-        peer = (row, toggled(col, k))
-        pair = [
-            pltpu.make_async_remote_copy(
+    gathers = [[], []]
+    for i, (src, dst) in enumerate(((coords_ref, cbuf), (half, pbuf))):
+        for k in range(1, groups):
+            copy = pltpu.make_async_remote_copy(
                 src_ref=src, dst_ref=dst.at[k - 1], send_sem=gs_sem.at[k - 1, i], recv_sem=gr_sem.at[k - 1, i],
-                device_id=peer, device_id_type=MESH,
+                device_id=(row, toggled(col, k)), device_id_type=MESH,
             )
-            for i, (src, dst) in enumerate(((coords_ref, cbuf), (half, pbuf)))
-        ]
-        for copy in pair:
             copy.start()
-        gathers.append(pair)
+            gathers[i].append(copy)
 
     at = lax.broadcasted_iota(jnp.int32, (8, LANES), 0)
     scales = jnp.ones((8, LANES), F32)
@@ -139,36 +135,49 @@
         kern = jnp.exp2(power)
         return kern, kern * (offset - slant * power)
 
-    def diagonal(feat, signs, first):
-        for j in range(0, width, LANES):
-            kern, slope = pair_of(j, feat)
-            both = jnp.concatenate([kern.astype(BF16), slope.astype(BF16)], axis=0)
-            got = dot_t(signs, both)
+    def diagonal_pairs(k, feat):
+        for j in range(width // LANES):
+            kern, slope = pair_of(j * LANES, feat)
+            near[k, j, :LANES, :] = kern.astype(BF16)
+            near[k, j, LANES:, :] = slope.astype(BF16)
+
+    def anchor_pairs(k, feat):
+        for level in range(levels):
+            kern, slope = pair_of(width + level * rank, feat)
+            for i, piece in enumerate(halves(kern) + halves(slope)):
+                fac[k, level, i * rank : (i + 1) * rank, :] = piece
+
+    def diagonal(k, signs):
+        for j in range(width // LANES):
+            got = dot_t(signs, near[k, j])
             for i in range(2):
                 part = got[:, i * LANES : (i + 1) * LANES]
-                if first:
-                    out_ref[i, :, j : j + LANES] = part
+                if k == 0:
+                    out_ref[i, :, j * LANES : (j + 1) * LANES] = part
                 else:
-                    out_ref[i, :, j : j + LANES] += part
-
-    def project(feat, signs, first):
-        for level in range(levels):
-            kern, slope = pair_of(width + level * rank, feat)
-            pieces = halves(kern) + halves(slope)
-            if first:
-                for i in range(4):
-                    fac[i, level] = pieces[i]
-            got = dot_t(signs, jnp.concatenate(pieces, axis=0))
+                    out_ref[i, :, j * LANES : (j + 1) * LANES] += part
+
+    def project(k, signs):
+        for level in range(levels - 1, -1, -1):
+            got = dot_t(signs, fac[k, level])
             for i in range(2):
                 part = got[:, 2 * i * rank : (2 * i + 1) * rank] + got[:, (2 * i + 1) * rank : (2 * i + 2) * rank]
-                if first:
+                if k == 0:
                     proj[level, i] = part
                 else:
                     proj[level, i] += part
 
     feat = features(coords_ref[...])
-    project(feat, half[...], True)
-    diagonal(feat, half[...], True)
+    anchor_pairs(0, feat)
+    diagonal_pairs(0, feat)
+    for k in range(1, groups):
+        gathers[0][k - 1].wait_recv()
+        feat = features(cbuf[k - 1])
+        anchor_pairs(k, feat)
+        diagonal_pairs(k, feat)
+
+    project(0, half[...])
+    diagonal(0, half[...])
 
     coupling = coup_ref[...]
     flipped = jnp.transpose(coupling)
@@ -178,30 +187,33 @@
         high, low = halves(core)
         both = jnp.concatenate([high, low], axis=0)
         for i in range(2):
-            got = dot(both, fac[2 * i, level])
-            total = got[:rank] + got[rank:] + dot(high, fac[2 * i + 1, level])
-            g_high, g_low = halves(total)
+            got = dot(both, fac[0, level, 2 * i * rank : (2 * i + 1) * rank, :])
+            rest = dot(high, fac[0, level, (2 * i + 1) * rank : (2 * i + 2) * rank, :])
+            g_high, g_low = halves(got[:rank] + got[rank:] + rest)
             grown[2 * i, level * rank : (level + 1) * rank, :] = g_high
             grown[2 * i + 1, level * rank : (level + 1) * rank, :] = g_low
 
     for k in range(1, groups):
-        for copy in gathers[k - 1]:
-            copy.wait_recv()
-        feat = features(cbuf[k - 1])
-        signs = pbuf[k - 1]
-        project(feat, signs, False)
+        gathers[1][k - 1].wait_recv()
+        project(k, pbuf[k - 1])
         if k < groups - 1:
-            diagonal(feat, signs, False)
-
-    send_a[...] = proj[...].astype(send_a.dtype)
-    swap = pltpu.make_async_remote_copy(
-        src_ref=send_a, dst_ref=recv_a, send_sem=as_sem, recv_sem=ar_sem,
-        device_id=(toggled(row, 1), col), device_id_type=MESH,
-    )
-    swap.start()
+            diagonal(k, pbuf[k - 1])
+
+    swaps = []
+    for i, (low, high) in enumerate(((1, levels), (0, 1))):
+        if high > low:
+            send_a[low:high] = proj[low:high].astype(send_a.dtype)
+            copy = pltpu.make_async_remote_copy(
+                src_ref=send_a.at[low:high], dst_ref=recv_a.at[low:high],
+                send_sem=as_sem.at[i], recv_sem=ar_sem.at[i],
+                device_id=(toggled(row, 1), col), device_id_type=MESH,
+            )
+            copy.start()
+            swaps.append(copy)
     if groups > 1:
-        diagonal(feat, signs, False)
-    swap.wait_recv()
+        diagonal(groups - 1, pbuf[groups - 2])
+    for copy in swaps[:-1]:
+        copy.wait_recv()
 
     send_b[...] = (proj[1:] + recv_a[1:].astype(F32)).astype(send_b.dtype)
     hops = []
@@ -225,6 +237,7 @@
         out_ref[0] += plain[:probes]
         out_ref[1] += plain[probes:] + c[:probes] + c[probes:] + d
 
+    swaps[-1].wait_recv()
     apply(jnp.concatenate([recv_a[0, 0], recv_a[0, 1]], axis=0).astype(F32), 0, rank)
     for copy in hops:
         copy.wait_recv()
@@ -239,11 +252,7 @@
     if sums:
         apply(jnp.concatenate(sums, axis=1), rank, levels * rank)
 
-    for pair in gathers:
-        for copy in pair:
-            copy.wait_send()
-    swap.wait_send()
-    for copy in hops:
+    for copy in gathers[0] + gathers[1] + swaps + hops:
         copy.wait_send()
 
 
@@ -260,7 +269,7 @@
     wire = F32
     return pl.pallas_call(
         functools.partial(kernel, groups, levels),
-        out_shape=jax.ShapeDtypeStruct((2, count, width), F32),
+        out_shape=pltpu.VMEM((2, count, width), F32),
         in_specs=[smem, smem, vmem, vmem, vmem, vmem],
         out_specs=vmem,
         scratch_shapes=[
@@ -268,7 +277,8 @@
             pltpu.VMEM((others, dims, width), jnp.int32),
             pltpu.VMEM((others, count, width), BF16),
             pltpu.VMEM((width + levels * rank, LANES), BF16),
-            pltpu.VMEM((4, levels, rank, width), BF16),
+            pltpu.VMEM((groups, width // LANES, 2 * LANES, width), BF16),
+            pltpu.VMEM((groups, levels, 4 * rank, width), BF16),
             pltpu.VMEM((4, levels * rank, width), BF16),
             pltpu.VMEM((levels, 2, count, rank), F32),
             pltpu.VMEM((levels, 2, count, rank), wire),
@@ -277,8 +287,8 @@
             pltpu.VMEM((hops, 2, count, rank), wire),
             pltpu.SemaphoreType.DMA((others, 2)),
             pltpu.SemaphoreType.DMA((others, 2)),
-            pltpu.SemaphoreType.DMA,
-            pltpu.SemaphoreType.DMA,
+            pltpu.SemaphoreType.DMA((2,)),
+            pltpu.SemaphoreType.DMA((2,)),
             pltpu.SemaphoreType.DMA((hops,)),
             pltpu.SemaphoreType.DMA((hops,)),
         ],

time: 27.1 us -> 23.8 us (0.88)
  Pallas kernels: 24.6 us -> 22.3 us
  local copies, waits for them, and re-layouts: 1.67 us -> 0.71 us
    pallas_call x1, Pallas kernels: 24.6 us -> 22.3 us  [on_device(): pl.pallas_call(functools.partial(kernel, groups, levels), out_shape=pltpu...]
    unnamed x1, local copies, waits for them, and re-layouts: 1.67 us -> 0.71 us
where the time goes in v2:
time: 23.8 us; the launch traced here: 23.7 us
  Pallas kernels  22.3 us (94%)
  local copies, waits for them, and re-layouts  0.71 us (3%)
  between operations  0.66 us (3%)
    pallas_call x1, Pallas kernels, on_device(): pl.pallas_call(functools.partial(kernel, groups, levels), out_shape=pltpu...  22.3 us
    unnamed x1, local copies, waits for them, and re-layouts  0.71 us

profile of v2, /device:TPU:0, one launch (start us, length us, event | category | flops | bytes accessed | tf_op | source)
XLA Modules:
  0.0 23.7 jit_solution(5881724225034447438)
XLA Ops:
  0.7 22.3 %shard_map.64 = f32[2,64,512]{2,1,0:T(8,128)S(1)} custom-call(f32[8]{0:T(128)} %scale_ref.1, f32[1]{0:T(128)S(6)} %copy.9.amp_ref, s32[8,512]{1,0:T(8,128)} %coords_ref.1, f32[64,512]{1,0:T(8,128)} %probes_ref.1, f32[14,8,128]{2,1,0:T(8,128)} %land_ref.1, f32[128,128]{1,0:T(8,128)} %coup_ref.1), custom_call_target="tpu_custom_call" | custom-call | tf_op jit(solution)/shard_map/pallas_call | solution.py:270
  23.0 0.7 %copy.8 = f32[2,64,512]{2,1,0:T(8,128)} copy(f32[2,64,512]{2,1,0:T(8,128)S(1)} %shard_map.64) | data formatting | bytes 524288

commit v3 on v2

--- a/solution.py
+++ b/solution.py
@@ -61,8 +61,8 @@
 
 def kernel(
     groups, levels,
-    scale_ref, amp_ref, coords_ref, probes_ref, land_ref, coup_ref, out_ref,
-    half, cbuf, pbuf, lhs, near, fac, grown, proj, send_a, recv_a, send_b, recv_b,
+    scale_hbm, amp_hbm, coords_hbm, probes_hbm, land_hbm, coup_hbm, out_ref,
+    scale_ref, amp_ref, coords_ref, probes_ref, land_ref, coup_ref, in_sem, half, cbuf, pbuf, lhs, near, fac, grown, proj, send_a, recv_a, send_b, recv_b,
     gs_sem, gr_sem, as_sem, ar_sem, bs_sem, br_sem,
 ):
     row, col = lax.axis_index("rows"), lax.axis_index("cols")
@@ -81,18 +81,31 @@
     barrier = pltpu.get_barrier_semaphore()
     for peer in peers:
         pl.semaphore_signal(barrier, inc=1, device_id=peer, device_id_type=MESH)
+    loads = [
+        pltpu.make_async_copy(src, dst, in_sem.at[i])
+        for i, (src, dst) in enumerate((
+            (probes_hbm, probes_ref), (coords_hbm, coords_ref), (scale_hbm, scale_ref),
+            (amp_hbm, amp_ref), (land_hbm, land_ref), (coup_hbm, coup_ref),
+        ))
+    ]
+    for load in loads:
+        load.start()
+    loads[1].wait()
+    loads[0].wait()
     half[...] = probes_ref[...].astype(BF16)
     pl.semaphore_wait(barrier, len(peers))
 
-    gathers = [[], []]
-    for i, (src, dst) in enumerate(((coords_ref, cbuf), (half, pbuf))):
+    gathers = {}
+    for part, (src, dst) in enumerate(((coords_ref, cbuf), (half, pbuf))):
         for k in range(1, groups):
-            copy = pltpu.make_async_remote_copy(
-                src_ref=src, dst_ref=dst.at[k - 1], send_sem=gs_sem.at[k - 1, i], recv_sem=gr_sem.at[k - 1, i],
+            gathers[k, part] = pltpu.make_async_remote_copy(
+                src_ref=src, dst_ref=dst.at[k - 1], send_sem=gs_sem.at[k - 1, part], recv_sem=gr_sem.at[k - 1, part],
                 device_id=(row, toggled(col, k)), device_id_type=MESH,
             )
-            copy.start()
-            gathers[i].append(copy)
+            gathers[k, part].start()
+
+    for load in loads[2:]:
+        load.wait()
 
     at = lax.broadcasted_iota(jnp.int32, (8, LANES), 0)
     scales = jnp.ones((8, LANES), F32)
@@ -171,7 +184,7 @@
     anchor_pairs(0, feat)
     diagonal_pairs(0, feat)
     for k in range(1, groups):
-        gathers[0][k - 1].wait_recv()
+        gathers[k, 0].wait_recv()
         feat = features(cbuf[k - 1])
         anchor_pairs(k, feat)
         diagonal_pairs(k, feat)
@@ -194,7 +207,7 @@
             grown[2 * i + 1, level * rank : (level + 1) * rank, :] = g_low
 
     for k in range(1, groups):
-        gathers[1][k - 1].wait_recv()
+        gathers[k, 1].wait_recv()
         project(k, pbuf[k - 1])
         if k < groups - 1:
             diagonal(k, pbuf[k - 1])
@@ -252,7 +265,7 @@
     if sums:
         apply(jnp.concatenate(sums, axis=1), rank, levels * rank)
 
-    for copy in gathers[0] + gathers[1] + swaps + hops:
+    for copy in list(gathers.values()) + swaps + hops:
         copy.wait_send()
 
 
@@ -265,14 +278,20 @@
     hops = max(2 ** (levels - 1) - 1, 1)
     upper = max(levels - 1, 1)
     vmem = pl.BlockSpec(memory_space=pltpu.VMEM)
-    smem = pl.BlockSpec(memory_space=pltpu.SMEM)
-    wire = F32
+    anywhere = pl.BlockSpec(memory_space=pl.ANY)
     return pl.pallas_call(
         functools.partial(kernel, groups, levels),
         out_shape=pltpu.VMEM((2, count, width), F32),
-        in_specs=[smem, smem, vmem, vmem, vmem, vmem],
+        in_specs=[anywhere] * 6,
         out_specs=vmem,
         scratch_shapes=[
+            pltpu.SMEM(lengthscales.shape, F32),
+            pltpu.SMEM(amplitude.shape, F32),
+            pltpu.VMEM(coords.shape, jnp.int32),
+            pltpu.VMEM(probes.shape, F32),
+            pltpu.VMEM(landmarks.shape, F32),
+            pltpu.VMEM(coupling.shape, F32),
+            pltpu.SemaphoreType.DMA((6,)),
             pltpu.VMEM((count, width), BF16),
             pltpu.VMEM((others, dims, width), jnp.int32),
             pltpu.VMEM((others, count, width), BF16),
@@ -281,10 +300,10 @@
             pltpu.VMEM((groups, levels, 4 * rank, width), BF16),
             pltpu.VMEM((4, levels * rank, width), BF16),
             pltpu.VMEM((levels, 2, count, rank), F32),
-            pltpu.VMEM((levels, 2, count, rank), wire),
-            pltpu.VMEM((levels, 2, count, rank), wire),
-            pltpu.VMEM((upper, 2, count, rank), wire),
-            pltpu.VMEM((hops, 2, count, rank), wire),
+            pltpu.VMEM((levels, 2, count, rank), F32),
+            pltpu.VMEM((levels, 2, count, rank), F32),
+            pltpu.VMEM((upper, 2, count, rank), BF16),
+            pltpu.VMEM((hops, 2, count, rank), BF16),
             pltpu.SemaphoreType.DMA((others, 2)),
             pltpu.SemaphoreType.DMA((others, 2)),
             pltpu.SemaphoreType.DMA((2,)),

time: 23.8 us -> 21.5 us (0.903)
  Pallas kernels: 22.3 us -> 20 us
    pallas_call x1, Pallas kernels: 22.3 us -> 20 us  [on_device(): pl.pallas_call(functools.partial(kernel, groups, levels), out_shape=pltpu...]
where the time goes in v3:
time: 21.5 us; the launch traced here: 21.4 us
  Pallas kernels  20 us (93%)
  local copies, waits for them, and re-layouts  0.71 us (3%)
  between operations  0.66 us (3%)
    pallas_call x1, Pallas kernels, on_device(): pl.pallas_call(functools.partial(kernel, groups, levels), out_shape=pltpu...  20 us
    unnamed x1, local copies, waits for them, and re-layouts  0.71 us

profile of v3, /device:TPU:0, one launch (start us, length us, event | category | flops | bytes accessed | tf_op | source)
XLA Modules:
  0.0 21.4 jit_solution(13166632259498125840)
XLA Ops:
  0.7 20.0 %shard_map.64 = f32[2,64,512]{2,1,0:T(8,128)S(1)} custom-call(f32[8]{0:T(128)} %scale_hbm.1, f32[1]{0:T(128)S(6)} %copy.9.amp_hbm, s32[8,512]{1,0:T(8,128)} %coords_hbm.1, f32[64,512]{1,0:T(8,128)} %probes_hbm.1, f32[14,8,128]{2,1,0:T(8,128)} %land_hbm.1, f32[128,128]{1,0:T(8,128)} %coup_hbm.1), custom_call_target="tpu_custom_call" | custom-call | tf_op jit(solution)/shard_map/pallas_call | solution.py:282
  20.7 0.7 %copy.8 = f32[2,64,512]{2,1,0:T(8,128)} copy(f32[2,64,512]{2,1,0:T(8,128)S(1)} %shard_map.64) | data formatting | bytes 524288

commit v4 on v3

--- a/solution.py
+++ b/solution.py
@@ -72,8 +72,8 @@
 
     targets = []
     for level in range(1, levels):
-        for m in range(2 ** (level - 1)):
-            targets.append((level, (1 << level) ^ (2 * m)))
+        for m in range(2**level):
+            targets.append((level, (1 << level) ^ m))
     peers = [(row, toggled(col, k)) for k in range(1, groups)]
     peers.append((toggled(row, 1), col))
     peers += [(toggled(row, mask), col) for _, mask in targets]
@@ -212,31 +212,23 @@
         if k < groups - 1:
             diagonal(k, pbuf[k - 1])
 
-    swaps = []
-    for i, (low, high) in enumerate(((1, levels), (0, 1))):
-        if high > low:
-            send_a[low:high] = proj[low:high].astype(send_a.dtype)
-            copy = pltpu.make_async_remote_copy(
-                src_ref=send_a.at[low:high], dst_ref=recv_a.at[low:high],
-                send_sem=as_sem.at[i], recv_sem=ar_sem.at[i],
-                device_id=(toggled(row, 1), col), device_id_type=MESH,
-            )
-            copy.start()
-            swaps.append(copy)
-    if groups > 1:
-        diagonal(groups - 1, pbuf[groups - 2])
-    for copy in swaps[:-1]:
-        copy.wait_recv()
-
-    send_b[...] = (proj[1:] + recv_a[1:].astype(F32)).astype(send_b.dtype)
+    send_b[...] = proj[1:].astype(send_b.dtype)
     hops = []
-    for i, (level, mask) in enumerate(targets):
+    for i, (level, mask) in reversed(list(enumerate(targets))):
         copy = pltpu.make_async_remote_copy(
             src_ref=send_b.at[level - 1], dst_ref=recv_b.at[i], send_sem=bs_sem.at[i], recv_sem=br_sem.at[i],
             device_id=(toggled(row, mask), col), device_id_type=MESH,
         )
         copy.start()
         hops.append(copy)
+    send_a[...] = proj[:1]
+    swap = pltpu.make_async_remote_copy(
+        src_ref=send_a, dst_ref=recv_a, send_sem=as_sem, recv_sem=ar_sem,
+        device_id=(toggled(row, 1), col), device_id_type=MESH,
+    )
+    swap.start()
+    if groups > 1:
+        diagonal(groups - 1, pbuf[groups - 2])
 
     def apply(sums, low_row, high_row):
         high, low = halves(sums)
@@ -250,7 +242,7 @@
         out_ref[0] += plain[:probes]
         out_ref[1] += plain[probes:] + c[:probes] + c[probes:] + d
 
-    swaps[-1].wait_recv()
+    swap.wait_recv()
     apply(jnp.concatenate([recv_a[0, 0], recv_a[0, 1]], axis=0).astype(F32), 0, rank)
     for copy in hops:
         copy.wait_recv()
@@ -265,7 +257,7 @@
     if sums:
         apply(jnp.concatenate(sums, axis=1), rank, levels * rank)
 
-    for copy in list(gathers.values()) + swaps + hops:
+    for copy in list(gathers.values()) + [swap] + hops:
         copy.wait_send()
 
 
@@ -275,10 +267,10 @@
     dims, width = coords.shape
     count, rank = probes.shape[0], coupling.shape[0]
     others = max(groups - 1, 1)
-    hops = max(2 ** (levels - 1) - 1, 1)
+    hops = max(2**levels - 2, 1)
     upper = max(levels - 1, 1)
     vmem = pl.BlockSpec(memory_space=pltpu.VMEM)
-    anywhere = pl.BlockSpec(memory_space=pl.ANY)
+    anywhere = pl.BlockSpec(memory_space=pltpu.HBM)
     return pl.pallas_call(
         functools.partial(kernel, groups, levels),
         out_shape=pltpu.VMEM((2, count, width), F32),
@@ -300,14 +292,14 @@
             pltpu.VMEM((groups, levels, 4 * rank, width), BF16),
             pltpu.VMEM((4, levels * rank, width), BF16),
             pltpu.VMEM((levels, 2, count, rank), F32),
-            pltpu.VMEM((levels, 2, count, rank), F32),
-            pltpu.VMEM((levels, 2, count, rank), F32),
+            pltpu.VMEM((1, 2, count, rank), F32),
+            pltpu.VMEM((1, 2, count, rank), F32),
             pltpu.VMEM((upper, 2, count, rank), BF16),
             pltpu.VMEM((hops, 2, count, rank), BF16),
             pltpu.SemaphoreType.DMA((others, 2)),
             pltpu.SemaphoreType.DMA((others, 2)),
-            pltpu.SemaphoreType.DMA((2,)),
-            pltpu.SemaphoreType.DMA((2,)),
+            pltpu.SemaphoreType.DMA,
+            pltpu.SemaphoreType.DMA,
             pltpu.SemaphoreType.DMA((hops,)),
             pltpu.SemaphoreType.DMA((hops,)),
         ],

time: 21.5 us -> 20.6 us (0.958)
  Pallas kernels: 20 us -> 19 us
    pallas_call x1, Pallas kernels: 20 us -> 19 us  [on_device(): pl.pallas_call(functools.partial(kernel, groups, levels), out_shape=pltpu...]
where the time goes in v4:
time: 20.6 us; the launch traced here: 20.4 us
  Pallas kernels  19 us (92%)
  local copies, waits for them, and re-layouts  0.71 us (3%)
  between operations  0.66 us (3%)
    pallas_call x1, Pallas kernels, on_device(): pl.pallas_call(functools.partial(kernel, groups, levels), out_shape=pltpu...  19 us
    unnamed x1, local copies, waits for them, and re-layouts  0.71 us

profile of v4, /device:TPU:0, one launch (start us, length us, event | category | flops | bytes accessed | tf_op | source)
XLA Modules:
  0.0 20.4 jit_solution(10198048199584064302)
XLA Ops:
  0.7 19.0 %shard_map.64 = f32[2,64,512]{2,1,0:T(8,128)S(1)} custom-call(f32[8]{0:T(128)} %scale_hbm.1, f32[1]{0:T(128)S(6)} %copy.9.amp_hbm, s32[8,512]{1,0:T(8,128)} %coords_hbm.1, f32[64,512]{1,0:T(8,128)} %probes_hbm.1, f32[14,8,128]{2,1,0:T(8,128)} %land_hbm.1, f32[128,128]{1,0:T(8,128)} %coup_hbm.1), custom_call_target="tpu_custom_call" | custom-call | tf_op jit(solution)/shard_map/pallas_call | solution.py:274
  19.7 0.7 %copy.8 = f32[2,64,512]{2,1,0:T(8,128)} copy(f32[2,64,512]{2,1,0:T(8,128)S(1)} %shard_map.64) | data formatting | bytes 524288
